TPU v7x, 32 devices: a whole 2x2x4 slice. The times are simulated.
32 devices in a mesh: depth: 8 (over y, x, core), tile: 4 (over z).
Axes of the slice: x: 2, y: 2, z: 4, core: 2. Of those that a mesh axis runs over, the one named last changes fastest.
Arguments:
- field: float32 [32, 384, 1024], P('depth', 'tile'), may hold values from -6 to 6
Outputs:
- image: float32 [4, 384, 1024], P(None, ('tile', 'depth'))
All inputs are finite; a program needn't handle non-finite values.
Results may differ from a plain program's by a relative error of at most 0.0003.
Values sent between devices are 32-bit elements; how exact they have to be, the bound alone decides.
A program may use at most 64 MiB of HBM per device.

v0:
```python
import jax
import jax.numpy as jnp
from jax import lax
from jax.sharding import PartitionSpec as P

centres = (-1.2, 0.3, 1.5)
spreads = (0.25, 0.35, 0.3)
heights = (2.0, 1.0, 3.0)
floor_density = 0.05
light_cols = 0.48
light_rows = 0.6
light_depth = 0.64


def from_behind(block, axis, distance):
    devices = range(lax.axis_size(axis))
    route = [(i - distance, i) for i in devices if i - distance in devices]
    return lax.ppermute(block, axis, route)


def extended(cells, sides, width):
    for axis, dim in sides:
        count = lax.axis_size(axis)
        ends = count - 1
        head = lax.slice_in_dim(cells, 0, width, axis=dim)
        tail = lax.slice_in_dim(cells, cells.shape[dim] - width, cells.shape[dim], axis=dim)
        cells = jnp.concatenate(
            [
                lax.ppermute(tail, axis, [(i, (i + 1) % count) for i in range(ends)]),
                cells,
                lax.ppermute(head, axis, [((i + 1) % count, i) for i in range(ends)]),
            ],
            axis=dim,
        )
    return cells


def swapped(value, axis, distance):
    mask = 2**distance
    pairs = [(source, source ^ mask) for source in range(lax.axis_size(axis))]
    return lax.ppermute(value, axis, pairs)


def emission(sample, slope_cols, slope_rows, slope_depth):
    density = floor_density + jnp.zeros_like(sample)
    for centre, spread, bump_height in zip(centres, spreads, heights):
        scaled = (sample - centre) / spread
        density = density + bump_height * jnp.exp(-scaled * scaled)
    facing = light_cols * slope_cols + light_rows * slope_rows + light_depth * slope_depth
    length = slope_cols * slope_cols + slope_rows * slope_rows + slope_depth * slope_depth + 1.0
    shading = 0.3 + 0.7 * jnp.abs(facing) * lax.rsqrt(length)
    colour = jnp.stack(
        [
            shading * jax.nn.sigmoid(2.0 * sample),
            shading * jnp.exp(-sample * sample),
            shading * jax.nn.sigmoid(-2.0 * sample),
        ]
    )
    return (density, colour)


def integrate(density, colour, spacing):
    optics = spacing * density
    running = jnp.cumsum(optics, axis=0)
    before = jnp.concatenate([jnp.zeros_like(optics[:1]), running[:-1]], axis=0)
    weight = jnp.exp(-before) * -jnp.expm1(-optics)
    return (jnp.sum(weight[None] * colour, axis=1), jnp.exp(-running[-1]))


def local(field):
    planes, row_count, col_count = field.shape
    depth_count = lax.axis_size("depth")
    spacing = 3.0 / (planes * depth_count)
    following = from_behind(field[:1], "depth", -1)
    further = jnp.concatenate([field[1:], following], axis=0)
    sample = 0.5 * (field + further)
    slope_depth = further - field
    edge_rows = jnp.concatenate([sample[:, :1], sample[:, -1:]], axis=1)
    edge_padded = extended(edge_rows, (("tile", 1),), 1)
    padded = jnp.concatenate([edge_padded[:, :1], sample, edge_padded[:, -1:]], axis=1)
    slope_rows = 0.5 * (padded[:, 2:] - padded[:, :-2])
    zero_col = jnp.zeros_like(sample[..., :1])
    slope_cols = 0.5 * (
        jnp.concatenate([sample[..., 1:], zero_col], axis=-1)
        - jnp.concatenate([zero_col, sample[..., :-1]], axis=-1)
    )
    density, colour = emission(sample, slope_cols, slope_rows, slope_depth)
    colour_sum, through = integrate(density, colour, spacing)
    row_share = row_count // depth_count
    colour_parts = colour_sum.reshape(3, depth_count, row_share, col_count)
    through_parts = through.reshape(1, depth_count, row_share, col_count)
    position = lax.axis_index("depth")
    rounds = depth_count.bit_length() - 1
    for round_bit in range(rounds):
        remaining = colour_parts.shape[1] // 2
        colour_pairs = colour_parts.reshape(3, remaining, 2, row_share, col_count)
        through_pairs = through_parts.reshape(1, remaining, 2, row_share, col_count)
        which_half = position >> round_bit & 1
        kept_colour = lax.dynamic_index_in_dim(colour_pairs, which_half, 2, False)
        sent_colour = lax.dynamic_index_in_dim(colour_pairs, 1 - which_half, 2, False)
        kept_through = lax.dynamic_index_in_dim(through_pairs, which_half, 2, False)
        sent_through = lax.dynamic_index_in_dim(through_pairs, 1 - which_half, 2, False)
        came_colour, came_through = swapped((sent_colour, sent_through), "depth", round_bit)
        in_front = which_half == 0
        colour_parts = jnp.where(
            in_front,
            kept_colour + kept_through * came_colour,
            came_colour + came_through * kept_colour,
        )
        through_parts = kept_through * came_through
    colour_out = colour_parts.reshape(3, row_share, col_count)
    through_out = through_parts.reshape(1, row_share, col_count)
    return jnp.concatenate([colour_out, 1.0 - through_out], axis=0)


def solution(mesh):
    return jax.shard_map(
        local,
        mesh=mesh,
        in_specs=(P("depth", "tile", None),),
        out_specs=P(None, ("tile", "depth"), None),
        check_vma=False,
    )
```

profile of v0, /device:TPU:0, one launch (start us, length us, event | category | flops | bytes accessed | tf_op | source)
XLA Modules:
  0.0 59.1 jit_solution(7478322179331381931)
XLA Ops:
  0.0 1.0 %slice.33 = f32[1,96,1024]{2,1,0:T(8,128)S(1)} slice(f32[4,96,1024]{2,1,0:T(8,128)} %param.1), slice={[0:1], [0:96], [0:1024]} | slice | bytes 786432 | tf_op jit(solution)/shard_map/slice | solution.py:74
  1.0 1.3 %collective-permute-start = (f32[1,96,1024]{2,1,0:T(8,128)S(1)}, f32[1,96,1024]{2,1,0:T(8,128)S(1)}, u32[]{:S(2)}, u32[]{:S(2)}) collective-permute-start(f32[1,96,1024]{2,1,0:T(8,128)S(1)} %slice.33), channel_id=1, source_target_pairs={{4,0},{8,4},{12,8},{16,12},{20,16},{24,20},{28,24},{5,1},{9,5},{13... | collective-permute-start | bytes 1179656 | tf_op jit(solution)/shard_map/ppermute | solution.py:18
  2.3 2.4 %slice.32 = f32[3,96,1024]{2,1,0:T(8,128)} slice(f32[4,96,1024]{2,1,0:T(8,128)} %param.1), slice={[1:4], [0:96], [0:1024]} | slice | bytes 2359296 | tf_op jit(solution)/shard_map/slice | solution.py:75
  4.7 0.0 collective-permute-done
  4.7 2.1 %broadcast_multiply_fusion = (f32[4,96,1024]{2,1,0:T(8,128)S(1)}, f32[4,96,1024]{2,1,0:T(8,128)S(1)}) fusion(f32[4,96,1024]{2,1,0:T(8,128)} %param.1, f32[1,96,1024]{2,1,0:T(8,128)S(1)} %collective-permute-done, f32[3,96,1024]{2,1,0:T(8,128)} %slice.32), kind=kLoop, calls=%fused_computation.27 | loop fusion | flops 1179648 | bytes 6291456 | tf_op jit(solution)/shard_map/mul | solution.py:76
  6.8 2.2 %fusion.24 = (f32[4,96,1023]{2,1,0:T(8,128)}, f32[4,96,1023]{2,1,0:T(8,128)}) fusion(f32[4,96,1024]{2,1,0:T(8,128)S(1)} %get-tuple-element.7), kind=kLoop, calls=%fused_computation.64 | loop fusion | bytes 6285312 | tf_op jit(solution)/shard_map/slice | solution.py:84
  9.1 0.6 %fusion.25 = (f32[4,1,1024]{2,1,0:T(1,128)}, f32[4,1,1024]{2,1,0:T(1,128)}) fusion(f32[4,96,1024]{2,1,0:T(8,128)S(1)} %get-tuple-element.7), kind=kLoop, calls=%fused_computation.65 | loop fusion | bytes 65536 | tf_op jit(solution)/shard_map/slice | solution.py:78
  9.7 1.3 %collective-permute-start.1 = (f32[4,1,1024]{2,1,0:T(1,128)}, f32[4,1,1024]{2,1,0:T(1,128)S(1)}, u32[]{:S(2)}, u32[]{:S(2)}) collective-permute-start(f32[4,1,1024]{2,1,0:T(1,128)} %get-tuple-element.16), channel_id=1, source_target_pairs={{1,0},{2,1},{3,2},{5,4},{6,5},{7,6},{9,8},{10,9},{11,10},{13,12},{... | collective-permute-start | bytes 49160 | tf_op jit(solution)/shard_map/ppermute | solution.py:31
  11.0 6.2 %collective-permute-start.2 = (f32[4,1,1024]{2,1,0:T(1,128)}, f32[4,1,1024]{2,1,0:T(1,128)}, u32[]{:S(2)}, u32[]{:S(2)}) collective-permute-start(f32[4,1,1024]{2,1,0:T(1,128)} %get-tuple-element.17), channel_id=1, source_target_pairs={{0,1},{1,2},{2,3},{4,5},{5,6},{6,7},{8,9},{9,10},{10,11},{12,13},{... | collective-permute-start | bytes 49160 | tf_op jit(solution)/shard_map/ppermute | solution.py:29
  17.2 1.5 %fusion.21 = f32[4,96,1024]{2,1,0:T(8,128)S(1)} fusion(f32[4,96,1024]{2,1,0:T(8,128)S(1)} %get-tuple-element.8), kind=kOutput, calls=%fused_computation.63 | output fusion | flops 8650752 | bytes 3145728 | tf_op jit(solution)/shard_map/jit(cumsum)/reduce_window_sum | solution.py:64
  18.7 0.8 %fusion.17 = f32[1,96,1024]{2,1,0:T(8,128)} fusion(f32[4,96,1024]{2,1,0:T(8,128)S(1)} %fusion.21), kind=kLoop, calls=%fused_computation.34 | loop fusion | flops 98304 | bytes 786432 | tf_op jit(solution)/shard_map/exp | solution.py:67
  19.5 1.1 %slice.42 = f32[3,96,1024]{2,1,0:T(8,128)} slice(f32[4,96,1024]{2,1,0:T(8,128)S(1)} %fusion.21), slice={[0:3], [0:96], [0:1024]} | slice | bytes 2359296 | tf_op jit(solution)/shard_map/slice | solution.py:65
  20.6 2.2 %exp.42 = f32[1,4,2,12,1024]{4,0,3,2,1:T(1,128)} reshape(f32[1,96,1024]{2,1,0:T(8,128)} %fusion.17) | data formatting | bytes 786432 | tf_op jit(solution)/shard_map/exp | solution.py:67
  22.8 0.0 collective-permute-done.1
  22.8 0.0 collective-permute-done.2
  22.8 4.0 %multiply_bitcast_fusion.1 = (f32[1,4,96,1024]{3,2,1,0:T(8,128)S(1)}, f32[4,96,1024]{2,1,0:T(8,128)S(1)}) fusion(f32[4,96,1024]{2,1,0:T(8,128)S(1)} %get-tuple-element.8, f32[4,96,1024]{2,1,0:T(8,128)} %param.1, f32[1,96,1024]{2,1,0:T(8,128)S(1)} %collective-permute-done, f32[3,96,1024]{2,1,0:T(8,128)} %slice.32, f32[4,96,1024]{2,1,0:T(8,128)S(1)} %get-tuple-element.7, ...), kind=kLoop, calls=%fused_computation.23 | loop fusion | flops 10616832 | bytes 12612608 | tf_op jit(solution)/shard_map/stack | solution.py:52
  26.8 2.4 %fusion.12 = (f32[1,4,96,1024]{3,2,1,0:T(8,128)S(1)}, f32[1,4,96,1024]{3,2,1,0:T(8,128)S(1)}, f32[4,96,1024]{2,1,0:T(8,128)S(1)}) fusion(f32[4,96,1024]{2,1,0:T(8,128)S(1)} %get-tuple-element.6, f32[4,96,1024]{2,1,0:T(8,128)S(1)} %get-tuple-element.8, f32[3,96,1024]{2,1,0:T(8,128)S(1)} %copy-done), kind=kLoop, calls=%fused_computation.17 | loop fusion | flops 12189696 | bytes 9043968 | tf_op jit(solution)/shard_map/stack | solution.py:52
  29.2 0.8 %fusion = f32[3,96,1024]{2,1,0:T(8,128)S(1)} fusion(f32[1,4,96,1024]{3,2,1,0:T(8,128)S(1)} %get-tuple-element.10, f32[1,4,96,1024]{3,2,1,0:T(8,128)S(1)} %get-tuple-element.9, f32[1,4,96,1024]{3,2,1,0:T(8,128)S(1)} %get-tuple-element.5, f32[4,96,1024]{2,1,0:T(8,128)S(1)} %get-tuple-element.13), kind=kLoop, calls=%fused_computation.1 | loop fusion | flops 4423680 | bytes 7471104 | tf_op jit(solution)/shard_map/reduce_sum | solution.py:67
  30.0 0.1 reshape_reshape.4
  30.2 0.2 constant_dynamic-slice_fusion.9
  30.4 0.4 copy.39
  30.7 5.2 %collective-permute-start.3 = (f32[3,4,12,1024]{3,1,2,0:T(4,128)S(1)}, f32[3,4,12,1024]{3,1,2,0:T(4,128)S(1)}, u32[]{:S(2)}, u32[]{:S(2)}) collective-permute-start(f32[3,4,12,1024]{3,1,2,0:T(4,128)S(1)} %bitcast.67), channel_id=1, source_target_pairs={{0,4},{4,0},{8,12},{12,8},{16,20},{20,16},{24,28},{28,24},{1,5},{5... | collective-permute-start | bytes 1769480 | tf_op jit(solution)/shard_map/ppermute | solution.py:41
  36.0 0.1 copy.42
  36.1 0.4 collective-permute-start.4
  36.5 0.1 copy.43
  36.6 1.2 %collective-permute-done.4 = f32[1,4,12,1024]{3,1,2,0:T(4,128)S(1)} collective-permute-done((f32[1,4,12,1024]{3,1,2,0:T(4,128)S(1)}, f32[1,4,12,1024]{3,1,2,0:T(4,128)S(1)}, u32[]{:S(2)}, u32[]{:S(2)}) %collective-permute-start.4) | collective-permute-done | bytes 196640 | tf_op jit(solution)/shard_map/ppermute | solution.py:41
  37.8 0.2 bitcast_multiply_fusion.2
  38.0 0.2 reshape.57
  38.2 0.2 constant_dynamic-slice_fusion.4
  38.4 0.7 %copy.44 = f32[1,2,1,12,1024]{4,3,1,2,0:T(8,128)} copy(f32[1,2,1,12,1024]{4,2,1,3,0:T(1,128)S(1)} %get-tuple-element.23) | data formatting | bytes 196608 | tf_op jit(solution)/shard_map/jit(dynamic_index_in_dim)/dynamic_slice | solution.py:102
  39.1 2.4 %collective-permute-start.6 = (f32[1,2,12,1024]{3,2,1,0:T(8,128)}, f32[1,2,12,1024]{3,2,1,0:T(8,128)}, u32[]{:S(2)}, u32[]{:S(2)}) collective-permute-start(f32[1,2,12,1024]{3,2,1,0:T(8,128)} %bitcast.61), channel_id=1, source_target_pairs={{0,8},{4,12},{8,0},{12,4},{16,24},{20,28},{24,16},{28,20},{1,9},{5... | collective-permute-start | bytes 294920 | tf_op jit(solution)/shard_map/ppermute | solution.py:41
  41.4 0.1 copy.45
  41.5 0.5 fusion.15
  42.0 0.5 reshape.56
  42.5 0.6 %constant_dynamic-slice_fusion.5 = (f32[3,2,1,12,1024]{4,2,1,3,0:T(1,128)S(1)}, f32[3,2,1,12,1024]{4,2,1,3,0:T(1,128)S(1)}) fusion(f32[3,2,2,12,1024]{4,2,1,3,0:T(2,128)S(1)} %reshape.56, s32[]{:T(128)S(6)} %select_n.60, s32[]{:T(128)S(6)} %select_n.61), kind=kLoop, calls=%fused_computation.58 | loop fusion | bytes 1179656 | tf_op jit(solution)/shard_map/jit(dynamic_index_in_dim)/dynamic_slice | solution.py:99
  43.1 0.2 copy.40
  43.2 0.1 collective-permute-start.5
  43.3 2.4 %collective-permute-done.6 = f32[1,2,12,1024]{3,2,1,0:T(8,128)} collective-permute-done((f32[1,2,12,1024]{3,2,1,0:T(8,128)}, f32[1,2,12,1024]{3,2,1,0:T(8,128)}, u32[]{:S(2)}, u32[]{:S(2)}) %collective-permute-start.6) | collective-permute-done | bytes 98336 | tf_op jit(solution)/shard_map/ppermute | solution.py:41
  45.8 0.9 %fusion.20 = f32[1,2,12,1024]{3,2,1,0:T(8,128)S(1)} fusion(f32[1,2,12,1024]{3,2,1,0:T(8,128)} %collective-permute-done.6, f32[1,2,1,12,1024]{4,2,1,3,0:T(1,128)S(1)} %get-tuple-element.22), kind=kLoop, calls=%fused_computation.47 | loop fusion | flops 24576 | bytes 294912 | tf_op jit(solution)/shard_map/mul | solution.py:110
  46.7 1.6 %collective-permute-start.8 = (f32[1,1,12,1024]{3,2,1,0:T(8,128)S(1)}, f32[1,1,12,1024]{3,2,1,0:T(8,128)S(1)}, u32[]{:S(2)}, u32[]{:S(2)}) collective-permute-start(f32[1,1,12,1024]{3,2,1,0:T(8,128)S(1)} %constant_dynamic-slice_fusion), channel_id=1, source_target_pairs={{0,16},{4,20},{8,24},{12,28},{16,0},{20,4},{24,8},{28,12},{1,17},{... | collective-permute-start | bytes 147464 | tf_op jit(solution)/shard_map/ppermute | solution.py:41
  48.3 1.0 %copy.46 = f32[1,2,12,1024]{3,1,2,0:T(2,128)S(1)} copy(f32[1,2,12,1024]{3,2,1,0:T(8,128)} %collective-permute-done.6) | data formatting | bytes 196608 | tf_op jit(solution)/shard_map/ppermute | solution.py:41
  49.3 3.0 %collective-permute-done.5 = f32[3,2,12,1024]{3,1,2,0:T(2,128)S(1)} collective-permute-done((f32[3,2,12,1024]{3,1,2,0:T(2,128)S(1)}, f32[3,2,12,1024]{3,1,2,0:T(2,128)S(1)}, u32[]{:S(2)}, u32[]{:S(2)}) %collective-permute-start.5) | collective-permute-done | bytes 294944 | tf_op jit(solution)/shard_map/ppermute | solution.py:41
  52.3 0.2 fusion.18
  52.6 0.1 constant_dynamic-slice_fusion.1
  52.7 0.6 %collective-permute-start.7 = (f32[3,1,12,1024]{3,1,2,0:T(1,128)S(1)}, f32[3,1,12,1024]{3,1,2,0:T(1,128)S(1)}, u32[]{:S(2)}, u32[]{:S(2)}) collective-permute-start(f32[3,1,12,1024]{3,1,2,0:T(1,128)S(1)} %constant_dynamic-slice_fusion.1), channel_id=1, source_target_pairs={{0,16},{4,20},{8,24},{12,28},{16,0},{20,4},{24,8},{28,12},{1,17},{... | collective-permute-start | bytes 442376 | tf_op jit(solution)/shard_map/ppermute | solution.py:41
  53.4 4.6 %collective-permute-done.7 = f32[3,1,12,1024]{3,1,2,0:T(1,128)S(1)} collective-permute-done((f32[3,1,12,1024]{3,1,2,0:T(1,128)S(1)}, f32[3,1,12,1024]{3,1,2,0:T(1,128)S(1)}, u32[]{:S(2)}, u32[]{:S(2)}) %collective-permute-start.7) | collective-permute-done | bytes 147488 | tf_op jit(solution)/shard_map/ppermute | solution.py:41
  57.9 0.3 broadcast_select_fusion
  58.3 0.8 %copy.19 = f32[4,12,1024]{2,0,1:T(4,128)} copy(f32[4,12,1024]{2,1,0:T(8,128)S(1)} %pad_maximum_fusion.3) | data formatting | bytes 393216 | tf_op jit(solution)/shard_map/concatenate | solution.py:113
  (11 shorter events, 0.1 us)
Async XLA Ops:
  1.0 3.7 %collective-permute-start = (f32[1,96,1024]{2,1,0:T(8,128)S(1)}, f32[1,96,1024]{2,1,0:T(8,128)S(1)}, u32[]{:S(2)}, u32[]{:S(2)}) collective-permute-start(f32[1,96,1024]{2,1,0:T(8,128)S(1)} %slice.33), channel_id=1, source_target_pairs={{4,0},{8,4},{12,8},{16,12},{20,16},{24,20},{28,24},{5,1},{9,5},{13... | collective-permute-start | bytes 1179656 | tf_op jit(solution)/shard_map/ppermute | solution.py:18
  9.7 13.1 %collective-permute-start.1 = (f32[4,1,1024]{2,1,0:T(1,128)}, f32[4,1,1024]{2,1,0:T(1,128)S(1)}, u32[]{:S(2)}, u32[]{:S(2)}) collective-permute-start(f32[4,1,1024]{2,1,0:T(1,128)} %get-tuple-element.16), channel_id=1, source_target_pairs={{1,0},{2,1},{3,2},{5,4},{6,5},{7,6},{9,8},{10,9},{11,10},{13,12},{... | collective-permute-start | bytes 49160 | tf_op jit(solution)/shard_map/ppermute | solution.py:31
  11.0 11.8 %collective-permute-start.2 = (f32[4,1,1024]{2,1,0:T(1,128)}, f32[4,1,1024]{2,1,0:T(1,128)}, u32[]{:S(2)}, u32[]{:S(2)}) collective-permute-start(f32[4,1,1024]{2,1,0:T(1,128)} %get-tuple-element.17), channel_id=1, source_target_pairs={{0,1},{1,2},{2,3},{4,5},{5,6},{6,7},{8,9},{9,10},{10,11},{12,13},{... | collective-permute-start | bytes 49160 | tf_op jit(solution)/shard_map/ppermute | solution.py:29
  22.8 4.0 %copy-start = (f32[3,96,1024]{2,1,0:T(8,128)S(1)}, f32[3,96,1024]{2,1,0:T(8,128)}, u32[]{:S(2)}) copy-start(f32[3,96,1024]{2,1,0:T(8,128)} %slice.42) | copy-start | bytes 3538948
  30.2 5.8 %copy-start.1 = (f32[1,4,2,12,1024]{4,0,3,2,1:T(1,128)S(1)}, f32[1,4,2,12,1024]{4,0,3,2,1:T(1,128)}, u32[]{:S(2)}) copy-start(f32[1,4,2,12,1024]{4,0,3,2,1:T(1,128)} %exp.42) | copy-start | bytes 1179652
  30.7 10.7 %collective-permute-start.3 = (f32[3,4,12,1024]{3,1,2,0:T(4,128)S(1)}, f32[3,4,12,1024]{3,1,2,0:T(4,128)S(1)}, u32[]{:S(2)}, u32[]{:S(2)}) collective-permute-start(f32[3,4,12,1024]{3,1,2,0:T(4,128)S(1)} %bitcast.67), channel_id=1, source_target_pairs={{0,4},{4,0},{8,12},{12,8},{16,20},{20,16},{24,28},{28,24},{1,5},{5... | collective-permute-start | bytes 1769480 | tf_op jit(solution)/shard_map/ppermute | solution.py:41
  36.1 1.7 %collective-permute-start.4 = (f32[1,4,12,1024]{3,1,2,0:T(4,128)S(1)}, f32[1,4,12,1024]{3,1,2,0:T(4,128)S(1)}, u32[]{:S(2)}, u32[]{:S(2)}) collective-permute-start(f32[1,4,12,1024]{3,1,2,0:T(4,128)S(1)} %bitcast.72), channel_id=1, source_target_pairs={{0,4},{4,0},{8,12},{12,8},{16,20},{20,16},{24,28},{28,24},{1,5},{5... | collective-permute-start | bytes 589832 | tf_op jit(solution)/shard_map/ppermute | solution.py:41
  39.1 6.7 %collective-permute-start.6 = (f32[1,2,12,1024]{3,2,1,0:T(8,128)}, f32[1,2,12,1024]{3,2,1,0:T(8,128)}, u32[]{:S(2)}, u32[]{:S(2)}) collective-permute-start(f32[1,2,12,1024]{3,2,1,0:T(8,128)} %bitcast.61), channel_id=1, source_target_pairs={{0,8},{4,12},{8,0},{12,4},{16,24},{20,28},{24,16},{28,20},{1,9},{5... | collective-permute-start | bytes 294920 | tf_op jit(solution)/shard_map/ppermute | solution.py:41
  43.2 9.1 %collective-permute-start.5 = (f32[3,2,12,1024]{3,1,2,0:T(2,128)S(1)}, f32[3,2,12,1024]{3,1,2,0:T(2,128)S(1)}, u32[]{:S(2)}, u32[]{:S(2)}) collective-permute-start(f32[3,2,12,1024]{3,1,2,0:T(2,128)S(1)} %bitcast.70), channel_id=1, source_target_pairs={{0,8},{4,12},{8,0},{12,4},{16,24},{20,28},{24,16},{28,20},{1,9},{5... | collective-permute-start | bytes 884744 | tf_op jit(solution)/shard_map/ppermute | solution.py:41
  46.7 6.6 %collective-permute-start.8 = (f32[1,1,12,1024]{3,2,1,0:T(8,128)S(1)}, f32[1,1,12,1024]{3,2,1,0:T(8,128)S(1)}, u32[]{:S(2)}, u32[]{:S(2)}) collective-permute-start(f32[1,1,12,1024]{3,2,1,0:T(8,128)S(1)} %constant_dynamic-slice_fusion), channel_id=1, source_target_pairs={{0,16},{4,20},{8,24},{12,28},{16,0},{20,4},{24,8},{28,12},{1,17},{... | collective-permute-start | bytes 147464 | tf_op jit(solution)/shard_map/ppermute | solution.py:41
  52.7 5.2 %collective-permute-start.7 = (f32[3,1,12,1024]{3,1,2,0:T(1,128)S(1)}, f32[3,1,12,1024]{3,1,2,0:T(1,128)S(1)}, u32[]{:S(2)}, u32[]{:S(2)}) collective-permute-start(f32[3,1,12,1024]{3,1,2,0:T(1,128)S(1)} %constant_dynamic-slice_fusion.1), channel_id=1, source_target_pairs={{0,16},{4,20},{8,24},{12,28},{16,0},{20,4},{24,8},{28,12},{1,17},{... | collective-permute-start | bytes 442376 | tf_op jit(solution)/shard_map/ppermute | solution.py:41
where the time goes:
time: 59.4 us; the launch traced here: 59.1 us
  starting transfers between devices  19 us (32%)
  local copies, waits for them, and re-layouts  14.9 us (25%)
  other arithmetic  13.7 us (23%)
  waiting for transfers between devices  11.2 us (19%)
    ppermute x6, waiting for transfers between devices, swapped(): return lax.ppermute(value, axis, pairs)  11.2 us
    ppermute x6, starting transfers between devices, swapped(): return lax.ppermute(value, axis, pairs)  10.3 us
    another operation x2, other arithmetic, emission(): jnp.stack([shading * jax.nn.sigmoid(2.0 * sample), shading * jnp.exp(-sam...  6.34 us
    ppermute x1, starting transfers between devices, extended(): lax.ppermute(tail, axis, [(i, (i + 1) % count) for i in range(ends)])  6.18 us
    slice x1, local copies, waits for them, and re-layouts, local(): further = jnp.concatenate([field[1:], following], axis=0)  2.42 us
    slice x1, local copies, waits for them, and re-layouts, local(): sample[..., 1:]  2.22 us
    exp x1, local copies, waits for them, and re-layouts, integrate(): return (jnp.sum(weight[None] * colour, axis=1), jnp.exp(-running[-1]))  2.2 us
    mul x1, other arithmetic, local(): sample = 0.5 * (field + further)  2.09 us
  transfers between devices with their start and end apart: 9, of which 4 were waited for; matrix products, arithmetic and copies ran while one was open for 23% of the time, Pallas kernels for 0%

commit v1 on v0

v1 whole, which is shorter than its diff:
```python
import functools
import math

import jax
import jax.numpy as jnp
from jax import lax
from jax.experimental import pallas as pl
from jax.experimental.pallas import tpu as pltpu
from jax.sharding import PartitionSpec as P

centres = (-1.2, 0.3, 1.5)
spreads = (0.25, 0.35, 0.3)
heights = (2.0, 1.0, 3.0)
floor_density = 0.05
light_cols = 0.48
light_rows = 0.6
light_depth = 0.64

LOG2E = math.log2(math.e)
SUB, LANE = 8, 128


def kernel(
    dims, field, out, raw, behind, grid, low_send, high_send, low, high,
    parts, pair, send, pieces, result,
    raw_sem, plane_sem, edge_send_sem, edge_recv_sem, pair_send_sem, pair_recv_sem,
    piece_send_sem, piece_recv_sem,
):
    planes, rows, cols, depth_count, tile_count = dims
    chips = depth_count // 2
    share = rows // depth_count
    spacing = 3.0 / (planes * depth_count)
    group = max(g for g in range(1, 5) if share % g == 0)
    me = lax.axis_index("depth")
    tile = lax.axis_index("tile")
    chip = me // 2
    core = me % 2
    partner = chip * 2 + (1 - core)

    def remote(src, dst, send_sem, recv_sem, depth_to, tile_to):
        return pltpu.make_async_remote_copy(
            src_ref=src, dst_ref=dst, send_sem=send_sem, recv_sem=recv_sem,
            device_id=(depth_to, tile_to), device_id_type=pl.DeviceIdType.MESH,
        )

    loads = [pltpu.make_async_copy(field.at[p], raw.at[p], raw_sem.at[p]) for p in range(planes)]
    for load in loads:
        load.start()

    has_front = me > 0
    has_behind = me < depth_count - 1
    has_low = tile > 0
    has_high = tile < tile_count - 1
    near = [
        (has_front, me - 1, tile),
        (has_behind, me + 1, tile),
        (has_low, me, tile - 1),
        (has_high, me, tile + 1),
        (has_front & has_low, me - 1, tile - 1),
        (has_front & has_high, me - 1, tile + 1),
        (has_behind & has_low, me + 1, tile - 1),
        (has_behind & has_high, me + 1, tile + 1),
    ]
    barrier = pltpu.get_barrier_semaphore()
    for cond, d, t in near:
        @pl.when(cond)
        def _(d=d, t=t):
            pl.semaphore_signal(barrier, inc=1, device_id=(d, t), device_id_type=pl.DeviceIdType.MESH)
    pl.semaphore_signal(barrier, inc=1, device_id=(partner, tile), device_id_type=pl.DeviceIdType.MESH)
    for step in range(chips - 1):
        other = (chip + step + 1) % chips * 2 + core
        pl.semaphore_signal(barrier, inc=1, device_id=(other, tile), device_id_type=pl.DeviceIdType.MESH)
    greeted = chips
    for cond, _, _ in near:
        greeted = greeted + cond.astype(jnp.int32)
    pl.semaphore_wait(barrier, greeted)

    front = remote(field.at[0], behind, plane_sem.at[0], plane_sem.at[1], me - 1, tile)

    @pl.when(has_front)
    def _():
        front.start()

    def spread(source, p):
        for r in range(0, rows, SUB):
            for j in range(cols // LANE):
                grid[p, pl.ds((r + 1) * SUB + j, SUB, stride=SUB), :] = source[
                    r : r + SUB, j * LANE : (j + 1) * LANE
                ]

    first, last = pl.ds(SUB, SUB), pl.ds(rows * SUB, SUB)
    for p in range(planes):
        loads[p].wait()
        spread(raw.at[p], p)
        low_send[p] = grid[p, first, :]
        high_send[p] = grid[p, last, :]
    own = pl.ds(0, planes)
    to_low = remote(low_send, high.at[own], edge_send_sem.at[0], edge_recv_sem.at[0], me, tile - 1)
    to_high = remote(high_send, low.at[own], edge_send_sem.at[1], edge_recv_sem.at[1], me, tile + 1)
    corner_low = remote(
        low_send.at[0], high.at[planes], edge_send_sem.at[2], edge_recv_sem.at[2], me - 1, tile - 1
    )
    corner_high = remote(
        high_send.at[0], low.at[planes], edge_send_sem.at[3], edge_recv_sem.at[3], me - 1, tile + 1
    )
    sends = [
        (has_low, to_low),
        (has_high, to_high),
        (has_front & has_low, corner_low),
        (has_front & has_high, corner_high),
    ]
    for cond, copy in sends:
        @pl.when(cond)
        def _(copy=copy):
            copy.start()

    below, above = pl.ds(0, SUB), pl.ds((rows + 1) * SUB, SUB)
    blank = jnp.zeros((SUB, LANE), jnp.float32)

    def fill(cond, copy, where, halo, which):
        @pl.when(cond)
        def _():
            copy.wait_recv()
            for p in which:
                grid[p, where, :] = halo[p]

        @pl.when(jnp.logical_not(cond))
        def _():
            for p in which:
                grid[p, where, :] = blank

    fill(has_high, to_low, above, high, range(planes))
    fill(has_low, to_high, below, low, range(planes))

    lane = lax.broadcasted_iota(jnp.int32, (group, SUB, LANE), 2)
    sub = lax.broadcasted_iota(jnp.int32, (group, SUB, LANE), 1)
    left_edge = lane == 0
    right_edge = lane == LANE - 1
    left_end = left_edge & (sub == 0)
    right_end = right_edge & (sub == SUB - 1)
    scale = spacing * LOG2E

    def plane_step(p, row, state):
        red, blue, green, through = state
        at = pl.ds(pl.multiple_of(row * SUB, SUB), (group + 2) * SUB)
        here = grid[p, at, :].reshape(group + 2, SUB, LANE)
        there = grid[p + 1, at, :].reshape(group + 2, SUB, LANE)
        total = here + there
        twice = total[1:-1]
        d_depth = there[1:-1] - here[1:-1]
        d_rows = total[2:] - total[:-2]
        from_left = pltpu.roll(twice, 1, 2)
        from_left = jnp.where(left_edge, pltpu.roll(from_left, 1, 1), from_left)
        from_left = jnp.where(left_end, 0.0, from_left)
        from_right = pltpu.roll(twice, LANE - 1, 2)
        from_right = jnp.where(right_edge, pltpu.roll(from_right, SUB - 1, 1), from_right)
        from_right = jnp.where(right_end, 0.0, from_right)
        d_cols = from_right - from_left
        facing = (0.25 * light_cols) * d_cols + (0.25 * light_rows) * d_rows + light_depth * d_depth
        length = (d_cols * d_cols + d_rows * d_rows) * 0.0625 + (d_depth * d_depth + 1.0)
        shading = 0.3 + 0.7 * jnp.abs(facing) * lax.rsqrt(length)
        optics = scale * floor_density
        for centre, width, bump in zip(centres, spreads, heights):
            root = math.sqrt(LOG2E) / width
            scaled = (0.5 * root) * twice - root * centre
            optics = optics + jnp.exp2(math.log2(bump * scale) - scaled * scaled)
        after = through * jnp.exp2(-optics)
        lit = (through - after) * shading
        middle = jnp.exp2((twice * (-0.25 * LOG2E)) * twice)
        balance = jnp.tanh(0.5 * twice)
        return (red + lit, blue + lit * balance, green + lit * middle, after)

    width = share * SUB

    def put(chunk, offset, state):
        at = pl.ds(pl.multiple_of(offset * SUB, SUB), group * SUB)
        for c in range(4):
            parts[chunk, c, at, :] = state[c].reshape(group * SUB, LANE)

    zero = jnp.zeros((group, SUB, LANE), jnp.float32)
    per_share = share // group

    def early(i, carry):
        state = (zero, zero, zero, zero + 1.0)
        for p in range(planes - 1):
            state = plane_step(p, i * group, state)
        put(i // per_share, i % per_share * group, state)
        return carry

    lax.fori_loop(0, rows // group, early, 0)

    @pl.when(has_behind)
    def _():
        front.wait_recv()
        spread(behind, planes)

    @pl.when(jnp.logical_not(has_behind))
    def _():
        grid[planes] = jnp.zeros(grid.shape[1:], jnp.float32)

    fill(has_behind & has_high, corner_low, above, high, (planes,))
    fill(has_behind & has_low, corner_high, below, low, (planes,))

    def late(chunk):
        def body(i, carry):
            at = pl.ds(pl.multiple_of(i * group * SUB, SUB), group * SUB)
            state = tuple(parts[chunk, c, at, :].reshape(group, SUB, LANE) for c in range(4))
            put(chunk, i * group, plane_step(planes - 1, chunk * share + i * group, state))
            return carry

        lax.fori_loop(0, per_share, body, 0)

    order = [(chip + step + 1) % chips for step in range(chips)]
    pair_copies = []
    for step, q in enumerate(order):
        chunk = q * 2 + (1 - core)
        late(chunk)
        copy = remote(parts.at[chunk], pair.at[step], pair_send_sem.at[step], pair_recv_sem.at[step], partner, tile)
        copy.start()
        pair_copies.append(copy)

    in_front = core == 0
    piece_copies = []
    for step, q in enumerate(order):
        chunk = q * 2 + core
        late(chunk)
        pair_copies[step].wait_recv()
        mine = [parts[chunk, c] for c in range(4)]
        theirs = [pair[step, c] for c in range(4)]
        near_through = jnp.where(in_front, mine[3], theirs[3])
        final = step == chips - 1
        target = pieces.at[chip] if final else send.at[step]
        for c in range(3):
            target[c] = jnp.where(in_front, mine[c], theirs[c]) + near_through * jnp.where(in_front, theirs[c], mine[c])
        target[3] = mine[3] * theirs[3]
        if not final:
            copy = remote(
                send.at[step], pieces.at[chip], piece_send_sem.at[step], piece_recv_sem.at[step],
                q * 2 + core, tile,
            )
            copy.start()
            piece_copies.append(copy)

    for copy in piece_copies:
        copy.wait_recv()
    colour = [pieces[0, c] for c in range(3)]
    through = pieces[0, 3]
    for k in range(1, chips):
        colour = [colour[c] + through * pieces[k, c] for c in range(3)]
        through = through * pieces[k, 3]
    result[0] = 0.5 * (colour[0] + colour[1])
    result[1] = colour[2]
    result[2] = 0.5 * (colour[0] - colour[1])
    result[3] = 1.0 - through
    for c in range(4):
        for j in range(cols // LANE):
            out[c, :, j * LANE : (j + 1) * LANE] = result[c, pl.ds(j, share, stride=SUB), :]

    for copy in pair_copies + piece_copies:
        copy.wait_send()
    for cond, copy in sends + [(has_front, front)]:
        @pl.when(cond)
        def _(copy=copy):
            copy.wait_send()


def local(field):
    planes, rows, cols = field.shape
    depth_count = lax.axis_size("depth")
    chips = depth_count // 2
    share = rows // depth_count
    f32 = jnp.float32
    dims = (planes, rows, cols, depth_count, lax.axis_size("tile"))
    dma = pltpu.SemaphoreType.DMA
    return pl.pallas_call(
        functools.partial(kernel, dims),
        out_shape=jax.ShapeDtypeStruct((4, share, cols), f32),
        in_specs=[pl.BlockSpec(memory_space=pl.ANY)],
        out_specs=pl.BlockSpec(memory_space=pltpu.VMEM),
        scratch_shapes=[
            pltpu.VMEM((planes, rows, cols), f32),
            pltpu.VMEM((rows, cols), f32),
            pltpu.VMEM((planes + 1, (rows + 2) * SUB, LANE), f32),
            pltpu.VMEM((planes, SUB, LANE), f32),
            pltpu.VMEM((planes, SUB, LANE), f32),
            pltpu.VMEM((planes + 1, SUB, LANE), f32),
            pltpu.VMEM((planes + 1, SUB, LANE), f32),
            pltpu.VMEM((depth_count, 4, share * SUB, LANE), f32),
            pltpu.VMEM((chips, 4, share * SUB, LANE), f32),
            pltpu.VMEM((chips, 4, share * SUB, LANE), f32),
            pltpu.VMEM((chips, 4, share * SUB, LANE), f32),
            pltpu.VMEM((4, share * SUB, LANE), f32),
            dma((planes,)),
            dma((2,)),
            dma((4,)),
            dma((4,)),
            dma((chips,)),
            dma((chips,)),
            dma((chips,)),
            dma((chips,)),
        ],
        compiler_params=pltpu.CompilerParams(collective_id=0, has_side_effects=True),
    )(field)


def solution(mesh):
    return jax.shard_map(
        local,
        mesh=mesh,
        in_specs=(P("depth", "tile", None),),
        out_specs=P(None, ("tile", "depth"), None),
        check_vma=False,
    )
```

time: 59.4 us -> 26 us (0.44)
  Pallas kernels: 0 us -> 24.1 us
  starting transfers between devices: 19 us -> 0 us
  other arithmetic: 13.7 us -> 0 us
  local copies, waits for them, and re-layouts: 14.9 us -> 1.76 us
  waiting for transfers between devices: 11.2 us -> 0 us
    pallas_call x0 -> x1, Pallas kernels: none -> 24.1 us  [local(): pl.pallas_call(functools.partial(kernel, dims), out_shape=jax.ShapeDtypeS...]
    ppermute x9 -> x0, starting transfers between devices: 19 us -> none  [the longest x6 10.3 us: swapped(): return lax.ppermute(value, axis, pairs)]
    ppermute x9 -> x0, waiting for transfers between devices: 11.2 us -> none  [the longest x6 11.2 us: swapped(): return lax.ppermute(value, axis, pairs)]
    another operation x3 -> x0, other arithmetic: 7.82 us -> none  [the longest x2 6.34 us: emission(): jnp.stack([shading * jax.nn.sigmoid(2.0 * sample), shading * jnp.exp(-sam...]
    slice x5 -> x0, local copies, waits for them, and re-layouts: 7.42 us -> none  [the longest x1 2.42 us: local(): further = jnp.concatenate([field[1:], following], axis=0)]
    mul x4 -> x0, other arithmetic: 3.2 us -> none  [the longest x1 2.09 us: local(): sample = 0.5 * (field + further)]
    dynamic_slice x8 -> x0, local copies, waits for them, and re-layouts: 2.34 us -> none  [the longest x2 0.82 us: local(): lax.dynamic_index_in_dim(through_pairs, 1 - which_half, 2, False)]
    exp x1 -> x0, local copies, waits for them, and re-layouts: 2.2 us -> none  [integrate(): return (jnp.sum(weight[None] * colour, axis=1), jnp.exp(-running[-1]))]
  transfers between devices with their start and end apart: 9 -> 0, of which waited for: 4 -> 0; matrix products, arithmetic and copies ran while one was open for 23% -> 0% of each run, Pallas kernels for 0% -> 0%
where the time goes in v1:
time: 26 us; the launch traced here: 25.9 us
  Pallas kernels  24.1 us (93%)
  local copies, waits for them, and re-layouts  1.76 us (7%)
    pallas_call x1, Pallas kernels, local(): pl.pallas_call(functools.partial(kernel, dims), out_shape=jax.ShapeDtypeS...  24.1 us
    pallas_call x1, local copies, waits for them, and re-layouts, local(): pl.pallas_call(functools.partial(kernel, dims), out_shape=jax.ShapeDtypeS...  1.76 us

profile of v1, /device:TPU:0, one launch (start us, length us, event | category | flops | bytes accessed | tf_op | source)
XLA Modules:
  0.0 25.9 jit_solution(12313368120161496101)
XLA Ops:
  0.0 24.1 %shard_map.17 = f32[4,12,1024]{2,1,0:T(8,128)} custom-call(f32[4,96,1024]{2,1,0:T(8,128)} %field.1), custom_call_target="tpu_custom_call" | custom-call | tf_op jit(solution)/shard_map/pallas_call | solution.py:275
  24.1 1.8 %copy.2 = f32[4,12,1024]{2,0,1:T(4,128)} copy(f32[4,12,1024]{2,1,0:T(8,128)} %shard_map.17) | data formatting | bytes 393216 | tf_op jit(solution)/shard_map/pallas_call | solution.py:275

commit v2 on v1

--- a/solution.py
+++ b/solution.py
@@ -23,7 +23,7 @@
 def kernel(
     dims, field, out, raw, behind, grid, low_send, high_send, low, high,
     parts, pair, send, pieces, result,
-    raw_sem, plane_sem, edge_send_sem, edge_recv_sem, pair_send_sem, pair_recv_sem,
+    raw_sem, plane_send_sem, plane_recv_sem, edge_send_sem, edge_recv_sem, pair_send_sem, pair_recv_sem,
     piece_send_sem, piece_recv_sem,
 ):
     planes, rows, cols, depth_count, tile_count = dims
@@ -70,17 +70,6 @@
     for step in range(chips - 1):
         other = (chip + step + 1) % chips * 2 + core
         pl.semaphore_signal(barrier, inc=1, device_id=(other, tile), device_id_type=pl.DeviceIdType.MESH)
-    greeted = chips
-    for cond, _, _ in near:
-        greeted = greeted + cond.astype(jnp.int32)
-    pl.semaphore_wait(barrier, greeted)
-
-    front = remote(field.at[0], behind, plane_sem.at[0], plane_sem.at[1], me - 1, tile)
-
-    @pl.when(has_front)
-    def _():
-        front.start()
-
     def spread(source, p):
         for r in range(0, rows, SUB):
             for j in range(cols // LANE):
@@ -94,6 +83,34 @@
         spread(raw.at[p], p)
         low_send[p] = grid[p, first, :]
         high_send[p] = grid[p, last, :]
+
+    greeted = chips
+    for cond, _, _ in near:
+        greeted = greeted + cond.astype(jnp.int32)
+    pl.semaphore_wait(barrier, greeted)
+
+    block = 2 * share
+    sends = []
+
+    def plane_row(row, count):
+        return grid.at[0, pl.ds(pl.multiple_of((row + 1) * SUB, SUB), count * SUB), :]
+
+    strips = []
+    for step in range(chips):
+        q = ((me + depth_count - 1) // 2 + step + 1) % chips
+        strip = []
+        for k, (cond, row, count, place) in enumerate((
+            (has_front, q * block, block, 1),
+            (has_front & (q > 0), jnp.maximum(q * block - 1, 0), 1, 0),
+            (has_front & (q < chips - 1), jnp.minimum((q + 1) * block, rows - 1), 1, block + 1),
+        )):
+            copy = remote(
+                plane_row(row, count), behind.at[step, pl.ds(place * SUB, count * SUB), :],
+                plane_send_sem.at[step, k], plane_recv_sem.at[step, k], me - 1, tile,
+            )
+            sends.append((cond, copy))
+            strip.append(copy)
+        strips.append(strip)
     own = pl.ds(0, planes)
     to_low = remote(low_send, high.at[own], edge_send_sem.at[0], edge_recv_sem.at[0], me, tile - 1)
     to_high = remote(high_send, low.at[own], edge_send_sem.at[1], edge_recv_sem.at[1], me, tile + 1)
@@ -103,13 +120,13 @@
     corner_high = remote(
         high_send.at[0], low.at[planes], edge_send_sem.at[3], edge_recv_sem.at[3], me - 1, tile + 1
     )
-    sends = [
+    edges = [
         (has_low, to_low),
         (has_high, to_high),
         (has_front & has_low, corner_low),
         (has_front & has_high, corner_high),
     ]
-    for cond, copy in sends:
+    for cond, copy in edges + sends:
         @pl.when(cond)
         def _(copy=copy):
             copy.start()
@@ -140,11 +157,11 @@
     right_end = right_edge & (sub == SUB - 1)
     scale = spacing * LOG2E
 
-    def plane_step(p, row, state):
+    def plane_step(p, row, state, there):
         red, blue, green, through = state
         at = pl.ds(pl.multiple_of(row * SUB, SUB), (group + 2) * SUB)
         here = grid[p, at, :].reshape(group + 2, SUB, LANE)
-        there = grid[p + 1, at, :].reshape(group + 2, SUB, LANE)
+        there = there.reshape(group + 2, SUB, LANE)
         total = here + there
         twice = total[1:-1]
         d_depth = there[1:-1] - here[1:-1]
@@ -180,51 +197,90 @@
     zero = jnp.zeros((group, SUB, LANE), jnp.float32)
     per_share = share // group
 
-    def early(i, carry):
-        state = (zero, zero, zero, zero + 1.0)
-        for p in range(planes - 1):
-            state = plane_step(p, i * group, state)
-        put(i // per_share, i % per_share * group, state)
-        return carry
-
-    lax.fori_loop(0, rows // group, early, 0)
-
-    @pl.when(has_behind)
-    def _():
-        front.wait_recv()
-        spread(behind, planes)
-
-    @pl.when(jnp.logical_not(has_behind))
-    def _():
-        grid[planes] = jnp.zeros(grid.shape[1:], jnp.float32)
-
-    fill(has_behind & has_high, corner_low, above, high, (planes,))
-    fill(has_behind & has_low, corner_high, below, low, (planes,))
-
-    def late(chunk):
+    def window(row):
+        return pl.ds(pl.multiple_of(row * SUB, SUB), (group + 2) * SUB)
+
+    order = [(chip + step + 1) % chips for step in range(chips)]
+
+    def early(step):
+        q = order[step]
+
+        def body(i, carry):
+            state = (zero, zero, zero, zero + 1.0)
+            row = q * block + i * group
+            for p in range(planes - 1):
+                state = plane_step(p, row, state, grid[p + 1, window(row), :])
+            put(q * 2 + i // per_share, i % per_share * group, state)
+            return carry
+
+        lax.fori_loop(0, block // group, body, 0)
+
+    def end(step, cond, have, copy, halo, place):
+        at = pl.ds(place * SUB, SUB)
+
+        @pl.when(cond & have)
+        def _():
+            copy.wait_recv()
+            behind[step, at, :] = halo[planes]
+
+        @pl.when(cond & jnp.logical_not(have))
+        def _():
+            behind[step, at, :] = blank
+
+    def arrive(step):
+        q = order[step]
+        whole, lower, upper = strips[step]
+
+        @pl.when(has_behind)
+        def _():
+            whole.wait_recv()
+
+        @pl.when(has_behind & (q > 0))
+        def _():
+            lower.wait_recv()
+
+        @pl.when(has_behind & (q < chips - 1))
+        def _():
+            upper.wait_recv()
+
+        end(step, has_behind & (q == 0), has_low, corner_high, low, 0)
+        end(step, has_behind & (q == chips - 1), has_high, corner_low, high, block + 1)
+
+        @pl.when(jnp.logical_not(has_behind))
+        def _():
+            behind[step] = jnp.zeros(behind.shape[1:], jnp.float32)
+
+    def late(step, side):
+        chunk = order[step] * 2 + side
+
         def body(i, carry):
             at = pl.ds(pl.multiple_of(i * group * SUB, SUB), group * SUB)
             state = tuple(parts[chunk, c, at, :].reshape(group, SUB, LANE) for c in range(4))
-            put(chunk, i * group, plane_step(planes - 1, chunk * share + i * group, state))
+            there = behind[step, window(side * share + i * group), :]
+            put(chunk, i * group, plane_step(planes - 1, chunk * share + i * group, state, there))
             return carry
 
         lax.fori_loop(0, per_share, body, 0)
 
-    order = [(chip + step + 1) % chips for step in range(chips)]
+    in_front = core == 0
     pair_copies = []
+    piece_copies = []
+    ahead = 2
+    for step in range(min(ahead, chips)):
+        early(step)
     for step, q in enumerate(order):
-        chunk = q * 2 + (1 - core)
-        late(chunk)
-        copy = remote(parts.at[chunk], pair.at[step], pair_send_sem.at[step], pair_recv_sem.at[step], partner, tile)
+        arrive(step)
+        late(step, 1 - core)
+        copy = remote(
+            parts.at[q * 2 + (1 - core)], pair.at[step], pair_send_sem.at[step], pair_recv_sem.at[step], partner, tile
+        )
         copy.start()
         pair_copies.append(copy)
-
-    in_front = core == 0
-    piece_copies = []
-    for step, q in enumerate(order):
+        late(step, core)
+        if step + ahead < chips:
+            early(step + ahead)
+        copy.wait_recv()
         chunk = q * 2 + core
-        late(chunk)
-        pair_copies[step].wait_recv()
         mine = [parts[chunk, c] for c in range(4)]
         theirs = [pair[step, c] for c in range(4)]
         near_through = jnp.where(in_front, mine[3], theirs[3])
@@ -248,17 +304,15 @@
     for k in range(1, chips):
         colour = [colour[c] + through * pieces[k, c] for c in range(3)]
         through = through * pieces[k, 3]
-    result[0] = 0.5 * (colour[0] + colour[1])
-    result[1] = colour[2]
-    result[2] = 0.5 * (colour[0] - colour[1])
-    result[3] = 1.0 - through
+    image = (0.5 * (colour[0] + colour[1]), colour[2], 0.5 * (colour[0] - colour[1]), 1.0 - through)
     for c in range(4):
-        for j in range(cols // LANE):
-            out[c, :, j * LANE : (j + 1) * LANE] = result[c, pl.ds(j, share, stride=SUB), :]
+        result[:, c * SUB : (c + 1) * SUB, :] = image[c].reshape(share, SUB, LANE)
+    for j in range(cols // LANE):
+        out[:, :, j * LANE : (j + 1) * LANE] = result[:, pl.ds(j, 4, stride=SUB), :]
 
     for copy in pair_copies + piece_copies:
         copy.wait_send()
-    for cond, copy in sends + [(has_front, front)]:
+    for cond, copy in edges + sends:
         @pl.when(cond)
         def _(copy=copy):
             copy.wait_send()
@@ -272,15 +326,15 @@
     f32 = jnp.float32
     dims = (planes, rows, cols, depth_count, lax.axis_size("tile"))
     dma = pltpu.SemaphoreType.DMA
-    return pl.pallas_call(
+    image = pl.pallas_call(
         functools.partial(kernel, dims),
-        out_shape=jax.ShapeDtypeStruct((4, share, cols), f32),
+        out_shape=jax.ShapeDtypeStruct((share, 4, cols), f32),
         in_specs=[pl.BlockSpec(memory_space=pl.ANY)],
         out_specs=pl.BlockSpec(memory_space=pltpu.VMEM),
         scratch_shapes=[
             pltpu.VMEM((planes, rows, cols), f32),
-            pltpu.VMEM((rows, cols), f32),
-            pltpu.VMEM((planes + 1, (rows + 2) * SUB, LANE), f32),
+            pltpu.VMEM((chips, (2 * share + 2) * SUB, LANE), f32),
+            pltpu.VMEM((planes, (rows + 2) * SUB, LANE), f32),
             pltpu.VMEM((planes, SUB, LANE), f32),
             pltpu.VMEM((planes, SUB, LANE), f32),
             pltpu.VMEM((planes + 1, SUB, LANE), f32),
@@ -289,9 +343,10 @@
             pltpu.VMEM((chips, 4, share * SUB, LANE), f32),
             pltpu.VMEM((chips, 4, share * SUB, LANE), f32),
             pltpu.VMEM((chips, 4, share * SUB, LANE), f32),
-            pltpu.VMEM((4, share * SUB, LANE), f32),
+            pltpu.VMEM((share, 4 * SUB, LANE), f32),
             dma((planes,)),
-            dma((2,)),
+            dma((chips, 3)),
+            dma((chips, 3)),
             dma((4,)),
             dma((4,)),
             dma((chips,)),
@@ -301,6 +356,7 @@
         ],
         compiler_params=pltpu.CompilerParams(collective_id=0, has_side_effects=True),
     )(field)
+    return jnp.transpose(image, (1, 0, 2))
 
 
 def solution(mesh):

time: 26 us -> 24.5 us (0.942)
  Pallas kernels: 24.1 us -> 22.7 us
    pallas_call x1 -> x0, local copies, waits for them, and re-layouts: 1.76 us -> none  [local(): pl.pallas_call(functools.partial(kernel, dims), out_shape=jax.ShapeDtypeS...]
    unnamed x0 -> x1, local copies, waits for them, and re-layouts: none -> 1.62 us
    pallas_call x1, Pallas kernels: 24.1 us -> 22.7 us  [local(): pl.pallas_call(functools.partial(kernel, dims), out_shape=jax.ShapeDtypeS...]
where the time goes in v2:
time: 24.5 us; the launch traced here: 24.3 us
  Pallas kernels  22.7 us (93%)
  local copies, waits for them, and re-layouts  1.62 us (7%)
    pallas_call x1, Pallas kernels, local(): pl.pallas_call(functools.partial(kernel, dims), out_shape=jax.ShapeDtypeS...  22.7 us
    unnamed x1, local copies, waits for them, and re-layouts  1.62 us

profile of v2, /device:TPU:0, one launch (start us, length us, event | category | flops | bytes accessed | tf_op | source)
XLA Modules:
  0.0 24.3 jit_solution(14346651429954677101)
XLA Ops:
  0.0 22.7 %shard_map.17 = f32[12,4,1024]{2,1,0:T(4,128)} custom-call(f32[4,96,1024]{2,1,0:T(8,128)} %field.1), custom_call_target="tpu_custom_call" | custom-call | tf_op jit(solution)/shard_map/pallas_call | solution.py:329
  22.7 1.6 %copy.3 = f32[4,12,1024]{2,0,1:T(4,128)} copy(f32[4,12,1024]{2,0,1:T(4,128)} %bitcast.1) | data formatting | bytes 393216

commit v3 on v2

--- a/solution.py
+++ b/solution.py
@@ -146,9 +146,6 @@
             for p in which:
                 grid[p, where, :] = blank
 
-    fill(has_high, to_low, above, high, range(planes))
-    fill(has_low, to_high, below, low, range(planes))
-
     lane = lax.broadcasted_iota(jnp.int32, (group, SUB, LANE), 2)
     sub = lax.broadcasted_iota(jnp.int32, (group, SUB, LANE), 1)
     left_edge = lane == 0
@@ -202,18 +199,12 @@
 
     order = [(chip + step + 1) % chips for step in range(chips)]
 
-    def early(step):
-        q = order[step]
-
-        def body(i, carry):
-            state = (zero, zero, zero, zero + 1.0)
-            row = q * block + i * group
-            for p in range(planes - 1):
-                state = plane_step(p, row, state, grid[p + 1, window(row), :])
-            put(q * 2 + i // per_share, i % per_share * group, state)
-            return carry
-
-        lax.fori_loop(0, block // group, body, 0)
+    def early(i, carry):
+        state = (zero, zero, zero, zero + 1.0)
+        for p in range(planes - 1):
+            state = plane_step(p, i * group, state, grid[p + 1, window(i * group), :])
+        put(i // per_share, i % per_share * group, state)
+        return carry
 
     def end(step, cond, have, copy, halo, place):
         at = pl.ds(place * SUB, SUB)
@@ -262,24 +253,19 @@
 
         lax.fori_loop(0, per_share, body, 0)
 
+    groups = rows // group
+    lax.fori_loop(1, groups - 1, early, 0)
+    fill(has_high, to_low, above, high, range(planes))
+    fill(has_low, to_high, below, low, range(planes))
+    lax.fori_loop(0, 2, lambda i, carry: early(i * (groups - 1), carry), 0)
+
     in_front = core == 0
     pair_copies = []
     piece_copies = []
-    ahead = 2
-    for step in range(min(ahead, chips)):
-        early(step)
-    for step, q in enumerate(order):
-        arrive(step)
-        late(step, 1 - core)
-        copy = remote(
-            parts.at[q * 2 + (1 - core)], pair.at[step], pair_send_sem.at[step], pair_recv_sem.at[step], partner, tile
-        )
-        copy.start()
-        pair_copies.append(copy)
-        late(step, core)
-        if step + ahead < chips:
-            early(step + ahead)
-        copy.wait_recv()
+
+    def combine(step):
+        q = order[step]
+        pair_copies[step].wait_recv()
         chunk = q * 2 + core
         mine = [parts[chunk, c] for c in range(4)]
         theirs = [pair[step, c] for c in range(4)]
@@ -297,6 +283,19 @@
             copy.start()
             piece_copies.append(copy)
 
+    for step, q in enumerate(order):
+        arrive(step)
+        late(step, 1 - core)
+        copy = remote(
+            parts.at[q * 2 + (1 - core)], pair.at[step], pair_send_sem.at[step], pair_recv_sem.at[step], partner, tile
+        )
+        copy.start()
+        pair_copies.append(copy)
+        late(step, core)
+        if step > 0:
+            combine(step - 1)
+    combine(chips - 1)
+
     for copy in piece_copies:
         copy.wait_recv()
     colour = [pieces[0, c] for c in range(3)]
@@ -304,7 +303,7 @@
     for k in range(1, chips):
         colour = [colour[c] + through * pieces[k, c] for c in range(3)]
         through = through * pieces[k, 3]
-    image = (0.5 * (colour[0] + colour[1]), colour[2], 0.5 * (colour[0] - colour[1]), 1.0 - through)
+    image = (0.5 * (colour[0] + colour[1]), colour[2], 0.5 * (colour[0] - colour[1]), through)
     for c in range(4):
         result[:, c * SUB : (c + 1) * SUB, :] = image[c].reshape(share, SUB, LANE)
     for j in range(cols // LANE):
@@ -356,7 +355,9 @@
         ],
         compiler_params=pltpu.CompilerParams(collective_id=0, has_side_effects=True),
     )(field)
-    return jnp.transpose(image, (1, 0, 2))
+    image = jnp.transpose(image, (1, 0, 2))
+    channel = lax.broadcasted_iota(jnp.int32, image.shape, 0)
+    return jnp.where(channel == 3, 1.0 - image, image)
 
 
 def solution(mesh):

time: 24.5 us -> 23.3 us (0.951)
  other arithmetic: 0 us -> 1.72 us
  local copies, waits for them, and re-layouts: 1.62 us -> 0 us
  Pallas kernels: 22.7 us -> 21.5 us
    select_n x0 -> x1, other arithmetic: none -> 1.71 us  [local(): return jnp.where(channel == 3, 1.0 - image, image)]
    unnamed x1 -> x0, local copies, waits for them, and re-layouts: 1.62 us -> none
    pallas_call x1, Pallas kernels: 22.7 us -> 21.5 us  [local(): pl.pallas_call(functools.partial(kernel, dims), out_shape=jax.ShapeDtypeS...]
where the time goes in v3:
time: 23.3 us; the launch traced here: 23.2 us
  Pallas kernels  21.5 us (92%)
  other arithmetic  1.72 us (7%)
    pallas_call x1, Pallas kernels, local(): pl.pallas_call(functools.partial(kernel, dims), out_shape=jax.ShapeDtypeS...  21.5 us
    select_n x1, other arithmetic, local(): return jnp.where(channel == 3, 1.0 - image, image)  1.71 us

profile of v3, /device:TPU:0, one launch (start us, length us, event | category | flops | bytes accessed | tf_op | source)
XLA Modules:
  0.0 23.2 jit_solution(12132338808932705025)
XLA Ops:
  0.0 21.5 %shard_map.17 = f32[12,4,1024]{2,1,0:T(4,128)} custom-call(f32[4,96,1024]{2,1,0:T(8,128)} %field.1), custom_call_target="tpu_custom_call" | custom-call | tf_op jit(solution)/shard_map/pallas_call | solution.py:328
  21.5 1.7 %subtract_select_fusion = f32[4,12,1024]{2,0,1:T(4,128)} fusion(f32[12,4,1024]{2,1,0:T(4,128)} %shard_map.17, pred[4]{0:T(512)(128)(4,1)S(1)} %iota_compare_fusion), kind=kLoop, calls=%fused_computation | loop fusion | flops 98304 | bytes 393220 | tf_op jit(solution)/shard_map/jit(_where)/select_n | solution.py:360
  (1 shorter events, 0.0 us)

commit v4 on v3

--- a/solution.py
+++ b/solution.py
@@ -328,7 +328,7 @@
     image = pl.pallas_call(
         functools.partial(kernel, dims),
         out_shape=jax.ShapeDtypeStruct((share, 4, cols), f32),
-        in_specs=[pl.BlockSpec(memory_space=pl.ANY)],
+        in_specs=[pl.BlockSpec(memory_space=pltpu.HBM)],
         out_specs=pl.BlockSpec(memory_space=pltpu.VMEM),
         scratch_shapes=[
             pltpu.VMEM((planes, rows, cols), f32),
@@ -353,7 +353,9 @@
             dma((chips,)),
             dma((chips,)),
         ],
-        compiler_params=pltpu.CompilerParams(collective_id=0, has_side_effects=True),
+        compiler_params=pltpu.CompilerParams(
+            collective_id=0, has_side_effects=True, vmem_limit_bytes=55_000_000
+        ),
     )(field)
     image = jnp.transpose(image, (1, 0, 2))
     channel = lax.broadcasted_iota(jnp.int32, image.shape, 0)

time: 23.3 us -> 21.7 us (0.931)
  other arithmetic: 1.72 us -> 0.79 us
  Pallas kernels: 21.5 us -> 20.8 us
    select_n x1, other arithmetic: 1.71 us -> 0.79 us  [local(): return jnp.where(channel == 3, 1.0 - image, image)]
    pallas_call x1, Pallas kernels: 21.5 us -> 20.8 us  [local(): pl.pallas_call(functools.partial(kernel, dims), out_shape=jax.ShapeDtypeS...]
where the time goes in v4:
time: 21.7 us; the launch traced here: 21.6 us
  Pallas kernels  20.8 us (96%)
  other arithmetic  0.79 us (4%)
    pallas_call x1, Pallas kernels, local(): pl.pallas_call(functools.partial(kernel, dims), out_shape=jax.ShapeDtypeS...  20.8 us
    select_n x1, other arithmetic, local(): return jnp.where(channel == 3, 1.0 - image, image)  0.79 us

profile of v4, /device:TPU:0, one launch (start us, length us, event | category | flops | bytes accessed | tf_op | source)
XLA Modules:
  0.0 21.6 jit_solution(10322942036984347555)
XLA Ops:
  0.0 20.8 %shard_map.17 = f32[12,4,1024]{2,1,0:T(4,128)S(1)} custom-call(f32[4,96,1024]{2,1,0:T(8,128)} %field.1), custom_call_target="tpu_custom_call" | custom-call | tf_op jit(solution)/shard_map/pallas_call | solution.py:328
  20.8 0.8 %subtract_select_fusion = f32[4,12,1024]{2,0,1:T(4,128)} fusion(f32[12,4,1024]{2,1,0:T(4,128)S(1)} %shard_map.17, pred[4]{0:T(512)(128)(4,1)S(1)} %iota_compare_fusion), kind=kLoop, calls=%fused_computation | loop fusion | flops 98304 | bytes 393220 | tf_op jit(solution)/shard_map/jit(_where)/select_n | solution.py:362
  (1 shorter events, 0.0 us)

commit v5 on v4

--- a/solution.py
+++ b/solution.py
@@ -95,9 +95,12 @@
     def plane_row(row, count):
         return grid.at[0, pl.ds(pl.multiple_of((row + 1) * SUB, SUB), count * SUB), :]
 
+    def turn(at, step):
+        return (at + (2 * (at % 2) - 1) * (step + 1) + chips) % chips
+
     strips = []
     for step in range(chips):
-        q = ((me + depth_count - 1) // 2 + step + 1) % chips
+        q = turn((me + depth_count - 1) // 2 % chips, step)
         strip = []
         for k, (cond, row, count, place) in enumerate((
             (has_front, q * block, block, 1),
@@ -197,7 +200,7 @@
     def window(row):
         return pl.ds(pl.multiple_of(row * SUB, SUB), (group + 2) * SUB)
 
-    order = [(chip + step + 1) % chips for step in range(chips)]
+    order = [turn(chip, step) for step in range(chips)]
 
     def early(i, carry):
         state = (zero, zero, zero, zero + 1.0)

time: 21.7 us -> 21.7 us (level)
  no operation moved by 1% of the time
where the time goes in v5:
time: 21.7 us; the launch traced here: 21.6 us
  Pallas kernels  20.8 us (96%)
  other arithmetic  0.79 us (4%)
    pallas_call x1, Pallas kernels, local(): pl.pallas_call(functools.partial(kernel, dims), out_shape=jax.ShapeDtypeS...  20.8 us
    select_n x1, other arithmetic, local(): return jnp.where(channel == 3, 1.0 - image, image)  0.79 us

profile of v5, /device:TPU:0, one launch (start us, length us, event | category | flops | bytes accessed | tf_op | source)
XLA Modules:
  0.0 21.6 jit_solution(2394169196359908020)
XLA Ops:
  0.0 20.8 %shard_map.17 = f32[12,4,1024]{2,1,0:T(4,128)S(1)} custom-call(f32[4,96,1024]{2,1,0:T(8,128)} %field.1), custom_call_target="tpu_custom_call" | custom-call | tf_op jit(solution)/shard_map/pallas_call | solution.py:331
  20.8 0.8 %subtract_select_fusion = f32[4,12,1024]{2,0,1:T(4,128)} fusion(f32[12,4,1024]{2,1,0:T(4,128)S(1)} %shard_map.17, pred[4]{0:T(512)(128)(4,1)S(1)} %iota_compare_fusion), kind=kLoop, calls=%fused_computation | loop fusion | flops 98304 | bytes 393220 | tf_op jit(solution)/shard_map/jit(_where)/select_n | solution.py:365
  (1 shorter events, 0.0 us)

commit v6 on v5

--- a/solution.py
+++ b/solution.py
@@ -78,12 +78,13 @@
                 ]
 
     first, last = pl.ds(SUB, SUB), pl.ds(rows * SUB, SUB)
-    for p in range(planes):
+    def settle(p):
         loads[p].wait()
         spread(raw.at[p], p)
         low_send[p] = grid[p, first, :]
         high_send[p] = grid[p, last, :]
 
+    settle(0)
     greeted = chips
     for cond, _, _ in near:
         greeted = greeted + cond.astype(jnp.int32)
@@ -114,6 +115,16 @@
             sends.append((cond, copy))
             strip.append(copy)
         strips.append(strip)
+
+    def launch(copies):
+        for cond, copy in copies:
+            @pl.when(cond)
+            def _(copy=copy):
+                copy.start()
+
+    launch(sends)
+    for p in range(1, planes):
+        settle(p)
     own = pl.ds(0, planes)
     to_low = remote(low_send, high.at[own], edge_send_sem.at[0], edge_recv_sem.at[0], me, tile - 1)
     to_high = remote(high_send, low.at[own], edge_send_sem.at[1], edge_recv_sem.at[1], me, tile + 1)
@@ -129,10 +140,7 @@
         (has_front & has_low, corner_low),
         (has_front & has_high, corner_high),
     ]
-    for cond, copy in edges + sends:
-        @pl.when(cond)
-        def _(copy=copy):
-            copy.start()
+    launch(edges)
 
     below, above = pl.ds(0, SUB), pl.ds((rows + 1) * SUB, SUB)
     blank = jnp.zeros((SUB, LANE), jnp.float32)

time: 21.7 us -> 22 us (1.014)
    pallas_call x1, Pallas kernels: 20.8 us -> 21 us  [local(): pl.pallas_call(functools.partial(kernel, dims), out_shape=jax.ShapeDtypeS...]
where the time goes in v6:
time: 22 us; the launch traced here: 21.8 us
  Pallas kernels  21 us (95%)
  other arithmetic  0.79 us (4%)
    pallas_call x1, Pallas kernels, local(): pl.pallas_call(functools.partial(kernel, dims), out_shape=jax.ShapeDtypeS...  21 us
    select_n x1, other arithmetic, local(): return jnp.where(channel == 3, 1.0 - image, image)  0.79 us

profile of v6, /device:TPU:0, one launch (start us, length us, event | category | flops | bytes accessed | tf_op | source)
XLA Modules:
  0.0 21.8 jit_solution(395618041727941091)
XLA Ops:
  0.0 21.0 %shard_map.17 = f32[12,4,1024]{2,1,0:T(4,128)S(1)} custom-call(f32[4,96,1024]{2,1,0:T(8,128)} %field.1), custom_call_target="tpu_custom_call" | custom-call | tf_op jit(solution)/shard_map/pallas_call | solution.py:339
  21.0 0.8 %subtract_select_fusion = f32[4,12,1024]{2,0,1:T(4,128)} fusion(f32[12,4,1024]{2,1,0:T(4,128)S(1)} %shard_map.17, pred[4]{0:T(512)(128)(4,1)S(1)} %iota_compare_fusion), kind=kLoop, calls=%fused_computation | loop fusion | flops 98304 | bytes 393220 | tf_op jit(solution)/shard_map/jit(_where)/select_n | solution.py:373
  (1 shorter events, 0.0 us)
